TPU v7x, 128 devices: a whole 4x4x4 slice. The times are simulated.
128 devices in a mesh: bin: 4 (over y), grp: 32 (over x, z, core).
Axes of the slice: x: 4, y: 4, z: 4, core: 2. Of those that a mesh axis runs over, the one named last changes fastest.
Arguments:
- templates: bfloat16 [131072, 512], P(('bin', 'grp')), may hold values from -6 to 6
- owner_device: int32 [131072, 1], P(('bin', 'grp')), may hold values from 0 to 127; in each aligned block of 1024 rows (0 to 1023, 1024 to 2047, ...) at most 16 rows name the same one
- rate_code: int32 [131072], P(('bin', 'grp')), may hold values from 0 to 4
- rate_gains: float32 [5, 512], replicated, may hold values from 0.5 to 2
- sketch: float32 [512, 256], replicated, may hold values from -6 to 6
- strain: float32 [2, 262144], P(None, 'grp'), may hold values from -6 to 6
Outputs:
- mixing: bfloat16 [131072, 256], P(('bin', 'grp'))
- spectrum: float32 [4, 256], P('bin')
- filtered_0: bfloat16 [4, 2, 262144, 256], P('bin', None, 'grp')
- filtered_1: bfloat16 [4, 2, 131072, 256], P('bin', None, 'grp')
- filtered_2: bfloat16 [4, 2, 65536, 256], P('bin', None, 'grp')
- filtered_3: bfloat16 [4, 2, 32768, 256], P('bin', None, 'grp')
- filtered_4: bfloat16 [4, 2, 16384, 256], P('bin', None, 'grp')
Inputs may be any that keep to these rules, and one draw needn't show every extreme that they name: `owner_device`: among the rows of one device, no device is named by more than 16 rows, and some device is named by exactly 16 rows.
All inputs are finite; a program needn't handle non-finite values.
Results may differ from a plain program's by a relative error of at most 0.0059.
Values may be sent and summed in bfloat16 or wider, within the bound.
A program may use at most 128 MiB of HBM per device.

v0:
```python
import math
import jax
import jax.numpy as jnp
from jax import lax
from jax.sharding import PartitionSpec as P

highest = lax.Precision.HIGHEST
inv_root_two = 0.7071067811865476


def shifted(x, axis, by):
    length = lax.axis_size(axis)
    pairs = [(i, i + by) for i in range(length) if 0 <= i + by < length]
    return lax.ppermute(x, axis, pairs)


def whiten_rows(templates, rate_code, rate_gains):
    factor = jnp.zeros(templates.shape, jnp.float32)
    for rate_level in range(rate_gains.shape[0]):
        factor = factor + jnp.where(
            (rate_code == rate_level)[:, None], rate_gains[rate_level][None, :], jnp.float32(0.0)
        )
    return (templates.astype(jnp.float32) * factor).astype(jnp.bfloat16)


def strain_levels(strain, count):
    current = strain
    level_list = []
    for rate_level in range(count):
        if rate_level > 0:
            paired = current.reshape(current.shape[0], -1, 2)
            current = (paired[:, :, 0] + paired[:, :, 1]) * inv_root_two
        level_list.append(current.astype(jnp.bfloat16))
    return level_list


def filter_level(history, rounded, basis_bf, stride):
    tap_rows = basis_bf[::stride]
    joined = jnp.concatenate([history[:, 1:], rounded], axis=1)
    return lax.conv_general_dilated(
        joined[:, :, None],
        tap_rows[::-1][:, None, :],
        (1,),
        "VALID",
        dimension_numbers=("NWC", "WIO", "NWC"),
        preferred_element_type=jnp.float32,
    )


def basis_from(product):
    inner_gram = jnp.dot(product.T, product, precision=highest)
    lower_factor = jnp.linalg.cholesky(inner_gram)
    basis_bf = jax.scipy.linalg.solve_triangular(lower_factor, product.T, lower=True).T.astype(
        jnp.bfloat16
    )
    return (basis_bf, jnp.diagonal(lower_factor))


def local(templates, owner_device, rate_code, rate_gains, sketch, strain):
    tpl_rows = templates.shape[0]
    slice_len = templates.shape[1]
    group_size = lax.axis_size("grp")
    bin_count = lax.axis_size("bin")
    devices = bin_count * group_size
    capacity = 2 * tpl_rows // devices
    scale_down = tpl_rows * group_size * math.sqrt(slice_len)
    whitened = whiten_rows(templates, rate_code, rate_gains)
    target = owner_device[:, 0]
    member_table = (target[:, None] == jnp.arange(devices, dtype=jnp.int32)[None, :]).astype(
        jnp.int32
    )
    rank_in_dest = jnp.sum(jnp.cumsum(member_table, axis=0) * member_table, axis=1) - 1
    slot_index = target * capacity + rank_in_dest
    outgoing = jnp.zeros((devices * capacity, slice_len), jnp.bfloat16).at[slot_index].set(whitened)
    received = lax.all_to_all(outgoing, ("bin", "grp"), split_axis=0, concat_axis=0, tiled=True)
    partial_gram = lax.dot_general(
        received, received, (((0,), (0,)), ((), ())), preferred_element_type=jnp.float32
    )
    gram_total = lax.psum(partial_gram, "grp")
    product = jnp.dot(gram_total, sketch, precision=highest)
    basis_bf, diag_here = basis_from(product)
    coeffs = jnp.dot(received, basis_bf, preferred_element_type=jnp.float32).astype(jnp.bfloat16)
    returned = lax.all_to_all(coeffs, ("bin", "grp"), split_axis=0, concat_axis=0, tiled=True)
    mixing = returned[slot_index]
    spectrum = (diag_here / scale_down)[None, :]
    levels = strain_levels(strain, rate_gains.shape[0])
    rim_list = [
        levels[rate_level][:, -(slice_len >> rate_level) :] for rate_level in range(len(levels))
    ]
    history = shifted((rim_list[0], rim_list[1], rim_list[2], rim_list[3], rim_list[4]), "grp", 1)
    filtered = []
    for rate_level in range(len(levels)):
        result_level = filter_level(
            history[rate_level], levels[rate_level], basis_bf, 2**rate_level
        )
        filtered.append(result_level.astype(jnp.bfloat16)[None])
    return (mixing, spectrum, filtered[0], filtered[1], filtered[2], filtered[3], filtered[4])


def solution(mesh):
    return jax.shard_map(
        local,
        mesh=mesh,
        in_specs=(
            P(("bin", "grp"), None),
            P(("bin", "grp"), None),
            P(("bin", "grp")),
            P(),
            P(),
            P(None, "grp"),
        ),
        out_specs=(
            P(("bin", "grp"), None),
            P("bin", None),
            P("bin", None, "grp", None),
            P("bin", None, "grp", None),
            P("bin", None, "grp", None),
            P("bin", None, "grp", None),
            P("bin", None, "grp", None),
        ),
        check_vma=False,
    )
```

profile of v0, /device:TPU:1, one launch (start us, length us, event | category | flops | bytes accessed | tf_op | source)
XLA Modules:
  0.0 488.1 jit_solution(5350892277837483940)
XLA Ops:
  9.0 7.3 %scatter_custom_fusion = bf16[2048,512]{1,0:T(8,128)(2,1)} fusion(s32[1024]{0:T(1024)S(1)} %bitcast.143, bf16[1024,512]{1,0:T(8,128)(2,1)S(1)} %copy-done.3, f32[512]{0:T(512)S(1)} %bitcast.149, f32[512]{0:T(512)S(1)} %bitcast.150, f32[512]{0:T(512)S(1)} %bitcast.147, f32[512]{0:T(512)S(1)} %bitcast.148, f32[]{:T(128)} %constant.105.clone.1, ...), kind=kCustom, calls=%fused_computation.26 | custom fusion | flops 6291456 | bytes 3161094 | tf_op jit(solution)/shard_map/scatter | solution.py:74
  16.3 12.0 %all-to-all-start = ((bf16[128,16,512]{2,1,0:T(8,128)(2,1)}), bf16[128,16,512]{2,1,0:T(8,128)(2,1)}, u32[]{:S(2)}, u32[]{:S(2)}) async-start(bf16[128,16,512]{2,1,0:T(8,128)(2,1)} %bitcast.12), calls=%async_computation | async-start | bytes 4194304 | tf_op jit(solution)/shard_map/all_to_all | solution.py:75
  28.4 3.7 collective-permute-start
  32.1 6.4 %reshape.114 = f32[2,4096,2]{2,1,0:T(8,128)} reshape(f32[2,8192]{1,0:T(2,128)S(1)} %copy-done.6) | data formatting | bytes 131072 | tf_op jit(solution)/shard_map/reshape | solution.py:31
  38.5 5.9 %convert_reduce_fusion = bf16[2,4096]{1,0:T(2,128)(2,1)S(1)} fusion(f32[2,4096,2]{2,1,0:T(8,128)} %reshape.114), kind=kLoop, calls=%fused_computation.17 | loop fusion | flops 24576 | bytes 81920 | tf_op jit(solution)/shard_map/convert_element_type | solution.py:33
  52.4 3.6 collective-permute-start.2
  71.7 4.5 convolution_bitcast_fusion
  78.0 104.7 %all-reduce.3.cloned.1.call-done = f32[512,512]{1,0:T(8,128)} async-done(((f32[512,512]{1,0:T(8,128)}), f32[512,512]{1,0:T(8,128)}) %all-reduce.3.cloned.1.call-update) | async-done | bytes 1048592 | tf_op jit(solution)/shard_map/psum | solution.py:79
  186.2 11.7 %cholesky.50 = f32[128,128]{1,0:T(8,128)S(1)} custom-call(f32[128,128]{1,0:T(8,128)S(1)} %cholesky.118), custom_call_target="Cholesky" | custom-call | tf_op jit(solution)/shard_map/jit(cholesky)/cholesky | solution.py:52
  197.9 9.8 %custom-call.15 = f32[1,128,128]{1,2,0:T(8,128)S(1)} custom-call(f32[1,128,128]{2,1,0:T(8,128)S(1)} %get-tuple-element.30), custom_call_target="InvertDiagBlocksLowerTriangular" | custom-call | tf_op jit(solution)/shard_map/jit(cholesky)/cholesky | solution.py:52
  208.2 12.2 %cholesky.105 = f32[128,128]{1,0:T(8,128)S(1)} custom-call(f32[128,128]{1,0:T(8,128)S(1)} %convolution_subtract_fusion.1), custom_call_target="Cholesky" | custom-call | tf_op jit(solution)/shard_map/jit(cholesky)/cholesky | solution.py:52
  222.5 4.0 while.1
  226.5 19.7 %custom-call.16 = f32[2,128,128]{1,2,0:T(8,128)S(1)} custom-call(f32[2,128,128]{2,1,0:T(8,128)S(1)} %get-tuple-element.14), custom_call_target="InvertDiagBlocksLowerTriangular" | custom-call | tf_op jit(solution)/shard_map/jit(_solve_triangular)/triangular_solve | solution.py:53
  248.5 6.6 %slice.147 = bf16[256,256]{0,1:T(8,128)(2,1)} slice(bf16[512,256]{0,1:T(8,128)(2,1)S(1)} %fusion.31), slice={[0:512:2], [0:256:1]} | slice | bytes 262144 | tf_op jit(solution)/shard_map/slice | solution.py:38
  261.3 3.3 convolution_convert_fusion
  264.6 8.5 %all-to-all-start.1 = ((bf16[128,16,256]{2,1,0:T(8,128)(2,1)}), bf16[128,16,256]{2,1,0:T(8,128)(2,1)}, u32[]{:S(2)}, u32[]{:S(2)}) async-start(bf16[128,16,256]{2,1,0:T(8,128)(2,1)} %bitcast.21), calls=%async_computation.1 | async-start | bytes 2097152 | tf_op jit(solution)/shard_map/all_to_all | solution.py:83
  276.4 123.6 %select_convert_fusion = bf16[16,1088,256]{2,0,1:T(8,128)(2,1)} fusion(pred[16,1088]{0,1:T(8,128)(4,1)S(1)} %bitcast.152, bf16[16,1599,1]{0,2,1:T(2,128)(2,1)S(1)} %copy.25, bf16[512,1,256]{2,1,0:T(2,128)(2,1)S(1)} %copy.26), kind=kOutput, calls=%fused_computation.5 | convolution fusion | flops 4572315648 | bytes 9243616 | tf_op jit(solution)/shard_map/conv_general_dilated | solution.py:40
  400.1 10.2 %copy.27 = bf16[16,1088,256]{2,1,0:T(8,128)(2,1)} copy(bf16[16,1088,256]{2,0,1:T(8,128)(2,1)} %select_convert_fusion) | data formatting | bytes 17825792 | tf_op jit(solution)/shard_map/convert_element_type | solution.py:96
  410.3 7.4 %slice_bitcast_fusion = bf16[1,2,8192,256]{3,2,1,0:T(8,128)(2,1)} fusion(bf16[2,8704,256]{2,1,0:T(8,128)(2,1)} %bitcast.129), kind=kLoop, calls=%fused_computation.7 | loop fusion | bytes 16777216 | tf_op jit(solution)/shard_map/broadcast_in_dim | solution.py:96
  418.3 31.3 %select_convert_fusion.1 = bf16[16,544,256]{2,0,1:T(8,128)(2,1)S(1)} fusion(pred[16,544]{0,1:T(8,128)(4,1)S(1)} %bitcast.153, bf16[16,799,1]{0,2,1:T(2,128)(2,1)S(1)} %copy-done.5, bf16[256,1,256]{2,1,0:T(2,128)(2,1)S(1)} %copy.29), kind=kOutput, calls=%fused_computation.6 | convolution fusion | flops 1145307136 | bytes 4621792 | tf_op jit(solution)/shard_map/conv_general_dilated | solution.py:40
  449.6 3.6 copy.30
  453.6 8.4 %select_convert_fusion.2 = bf16[16,272,256]{2,0,1:T(8,128)(2,1)S(1)} fusion(pred[16,272]{0,1:T(8,128)(4,1)S(1)} %copy-done.19, bf16[16,399,1]{0,2,1:T(2,128)(2,1)S(1)} %copy-done.10, bf16[128,1,256]{2,1,0:T(2,128)(2,1)S(1)} %copy.32), kind=kOutput, calls=%fused_computation.8 | convolution fusion | flops 287440896 | bytes 2310880 | tf_op jit(solution)/shard_map/conv_general_dilated | solution.py:40
  470.6 4.5 slice_bitcast_fusion.1
  475.0 6.0 %gather_fusion = bf16[1024,256]{1,0:T(8,128)(2,1)} fusion(bf16[2048,256]{1,0:T(8,128)(2,1)} %bitcast.22, s32[1024]{0:T(1024)S(1)} %copy-done.14), kind=kCustom, calls=%fused_computation | custom fusion | bytes 1052672 | tf_op jit(solution)/shard_map/gather | solution.py:84
  (169 shorter events, 57.0 us)
Async XLA Ops:
  7.2 175.5 %copy-start = (f32[512,256]{1,0:T(8,128)S(1)}, f32[512,256]{1,0:T(8,128)}, u32[]{:S(2)}) copy-start(f32[512,256]{1,0:T(8,128)} %param.10) | copy-start | bytes 1572868
  7.2 1.8 copy-start.16
  7.2 1.8 copy-start.3
  16.3 12.0 %copy-start.6 = (f32[2,8192]{1,0:T(2,128)S(1)}, f32[2,8192]{1,0:T(2,128)}, u32[]{:S(2)}) copy-start(f32[2,8192]{1,0:T(2,128)} %param.11) | copy-start | bytes 196612
  16.3 55.3 %all-to-all-start = ((bf16[128,16,512]{2,1,0:T(8,128)(2,1)}), bf16[128,16,512]{2,1,0:T(8,128)(2,1)}, u32[]{:S(2)}, u32[]{:S(2)}) async-start(bf16[128,16,512]{2,1,0:T(8,128)(2,1)} %bitcast.12), calls=%async_computation | async-start | bytes 4194304 | tf_op jit(solution)/shard_map/all_to_all | solution.py:75
  28.3 154.4 %all-reduce.3.cloned.1.call-start = ((), (), s32[]{:S(2)}) async-start(), calls=%async_computation.2 | async-start | bytes 2097152 | tf_op jit(solution)/shard_map/psum | solution.py:79
  28.4 43.2 %collective-permute-start = (bf16[2,512]{1,0:T(2,128)(2,1)S(1)}, bf16[2,512]{1,0:T(2,128)(2,1)S(1)}, u32[]{:S(2)}, u32[]{:S(2)}) collective-permute-start(bf16[2,512]{1,0:T(2,128)(2,1)S(1)} %slice.190), channel_id=1, source_target_pairs={{0,1},{1,2},{2,3},{3,4},{4,5},{5,6},{6,7},{7,8},{8,9},{9,10},{10,1... | collective-permute-start | bytes 6152 | tf_op jit(solution)/shard_map/ppermute | solution.py:14
  38.5 8.1 %copy-start.2 = (f32[2,4096,2]{2,1,0:T(8,128)S(1)}, f32[2,4096,2]{2,1,0:T(8,128)}, u32[]{:S(2)}) copy-start(f32[2,4096,2]{2,1,0:T(8,128)} %reshape.114) | copy-start | bytes 196612
  44.4 25.7 %collective-permute-start.1 = (bf16[2,256]{1,0:T(2,128)(2,1)S(1)}, bf16[2,256]{1,0:T(2,128)(2,1)S(1)}, u32[]{:S(2)}, u32[]{:S(2)}) collective-permute-start(bf16[2,256]{1,0:T(2,128)(2,1)S(1)} %slice.196), channel_id=1, source_target_pairs={{0,1},{1,2},{2,3},{3,4},{4,5},{5,6},{6,7},{7,8},{8,9},{9,10},{10,1... | collective-permute-start | bytes 3080 | tf_op jit(solution)/shard_map/ppermute | solution.py:14
  52.4 16.5 %collective-permute-start.2 = (bf16[2,128]{1,0:T(2,128)(2,1)S(1)}, bf16[2,128]{1,0:T(2,128)(2,1)S(1)}, u32[]{:S(2)}, u32[]{:S(2)}) collective-permute-start(bf16[2,128]{1,0:T(2,128)(2,1)S(1)} %slice.202), channel_id=1, source_target_pairs={{0,1},{1,2},{2,3},{3,4},{4,5},{5,6},{6,7},{7,8},{8,9},{9,10},{10,1... | collective-permute-start | bytes 1544 | tf_op jit(solution)/shard_map/ppermute | solution.py:14
  59.0 8.8 %collective-permute-start.3 = (bf16[2,64]{1,0:T(2,128)(2,1)S(1)}, bf16[2,64]{1,0:T(2,128)(2,1)S(1)}, u32[]{:S(2)}, u32[]{:S(2)}) collective-permute-start(bf16[2,64]{1,0:T(2,128)(2,1)S(1)} %slice.207), channel_id=1, source_target_pairs={{0,1},{1,2},{2,3},{3,4},{4,5},{5,6},{6,7},{7,8},{8,9},{9,10},{10,1... | collective-permute-start | bytes 776 | tf_op jit(solution)/shard_map/ppermute | solution.py:14
  62.7 4.0 collective-permute-start.4
  264.6 11.8 %copy-start.17 = (pred[16,1088]{0,1:T(32,128)(4,1)S(1)}, pred[16,1088]{0,1:T(32,128)(4,1)}, u32[]{:S(2)}) copy-start(pred[16,1088]{0,1:T(32,128)(4,1)} %constant.152) | copy-start | bytes 52228
  264.6 210.4 %all-to-all-start.1 = ((bf16[128,16,256]{2,1,0:T(8,128)(2,1)}), bf16[128,16,256]{2,1,0:T(8,128)(2,1)}, u32[]{:S(2)}, u32[]{:S(2)}) async-start(bf16[128,16,256]{2,1,0:T(8,128)(2,1)} %bitcast.21), calls=%async_computation.1 | async-start | bytes 2097152 | tf_op jit(solution)/shard_map/all_to_all | solution.py:83
  410.3 7.4 %copy-start.4 = (bf16[256,256]{0,1:T(8,128)(2,1)S(1)}, bf16[256,256]{0,1:T(8,128)(2,1)}, u32[]{:S(2)}) copy-start(bf16[256,256]{0,1:T(8,128)(2,1)} %slice.147) | copy-start | bytes 393220
  410.3 8.0 %copy-start.5 = (bf16[16,799,1]{0,2,1:T(2,128)(2,1)S(1)}, bf16[16,799,1]{0,2,1:T(2,128)(2,1)}, u32[]{:S(2)}) copy-start(bf16[16,799,1]{0,2,1:T(2,128)(2,1)} %copy.28) | copy-start | bytes 76708
  410.3 8.0 %copy-start.18 = (pred[16,544]{0,1:T(32,128)(4,1)S(1)}, pred[16,544]{0,1:T(32,128)(4,1)}, u32[]{:S(2)}) copy-start(pred[16,544]{0,1:T(32,128)(4,1)} %constant.153) | copy-start | bytes 26116
  449.6 3.7 copy-start.9
  449.6 4.0 copy-start.10
  449.6 4.0 copy-start.19
  462.7 1.8 copy-start.11
  462.8 1.8 copy-start.20
  470.6 4.5 copy-start.14
  475.0 6.0 %copy-start.1 = (f32[512,256]{1,0:T(8,128)S(1)}, f32[512,256]{1,0:T(8,128)}, u32[]{:S(2)}) copy-start(f32[512,256]{1,0:T(8,128)} %param.10) | copy-start | bytes 1572868
  (6 other events, 9.5 us)
Sparse Core Ops, SparseCore 0:
  76.3 106.3 all-reduce.2
where the time goes:
time: 496 us; the launch traced here: 488 us
  matrix products  179 us (36%)
  waiting for transfers between devices  105 us (21%)
  other arithmetic  76.5 us (15%)
  local copies, waits for them, and re-layouts  75.8 us (15%)
  starting transfers between devices  35.3 us (7%)
  between operations  16.3 us (3%)
    conv_general_dilated x5, matrix products, filter_level(): lax.conv_general_dilated(joined[:, :, None], tap_rows[::-1][:, None, :],...  166 us
    psum x1, waiting for transfers between devices, local(): gram_total = lax.psum(partial_gram, 'grp')  105 us
    another operation x6, other arithmetic, basis_from(): lower_factor = jnp.linalg.cholesky(inner_gram)  34.4 us
    another operation x3, other arithmetic, basis_from(): jax.scipy.linalg.solve_triangular(lower_factor, product.T, lower=True)  19.7 us
    convert_element_type x6, local copies, waits for them, and re-layouts, local(): filtered.append(result_level.astype(jnp.bfloat16)[None])  15.2 us
    broadcast_in_dim x5, local copies, waits for them, and re-layouts, local(): filtered.append(result_level.astype(jnp.bfloat16)[None])  15.2 us
    ppermute x5, starting transfers between devices, shifted(): return lax.ppermute(x, axis, pairs)  14.9 us
    slice x4, local copies, waits for them, and re-layouts, filter_level(): tap_rows = basis_bf[::stride]  12.8 us
  transfers between devices with their start and end apart: 8, of which 2 were waited for; matrix products, arithmetic and copies ran while one was open for 47% of the time, Pallas kernels for 0%

commit v1 on v0

--- a/solution.py
+++ b/solution.py
@@ -6,6 +6,19 @@
 
 highest = lax.Precision.HIGHEST
 inv_root_two = 0.7071067811865476
+
+
+def arrange_tracks_by_axis(x_local):
+    total_devices = lax.psum(1, "grp")
+    mixed_arr, z1 = (x_local, 0)
+    while 1 << z1 < total_devices:
+        line_up = []
+        for dev_j in range(total_devices):
+            line_up.append((dev_j, dev_j ^ 1 << z1))
+        d_next = lax.ppermute(mixed_arr, "grp", line_up)
+        mixed_arr = mixed_arr + d_next
+        z1 = z1 + 1
+    return mixed_arr
 
 
 def shifted(x, axis, by):
@@ -76,7 +89,7 @@
     partial_gram = lax.dot_general(
         received, received, (((0,), (0,)), ((), ())), preferred_element_type=jnp.float32
     )
-    gram_total = lax.psum(partial_gram, "grp")
+    gram_total = arrange_tracks_by_axis(partial_gram)
     product = jnp.dot(gram_total, sketch, precision=highest)
     basis_bf, diag_here = basis_from(product)
     coeffs = jnp.dot(received, basis_bf, preferred_element_type=jnp.float32).astype(jnp.bfloat16)

time: 496 us -> 480 us (0.968)
  blocking collectives: 0 us -> 41.5 us
  waiting for transfers between devices: 105 us -> 66.8 us
  between operations: 16.3 us -> 2.93 us
  starting transfers between devices: 35.3 us -> 27.9 us
  other arithmetic: 76.5 us -> 82 us
  matrix products: 179 us -> 174 us
    psum x1 -> x0, waiting for transfers between devices: 105 us -> none  [local(): gram_total = lax.psum(partial_gram, 'grp')]
    ppermute x0 -> x5, waiting for transfers between devices: none -> 50.8 us  [arrange_tracks_by_axis(): d_next = lax.ppermute(mixed_arr, 'grp', line_up)]
    all_to_all x0 -> x1, blocking collectives: none -> 41.5 us  [local(): lax.all_to_all(outgoing, ('bin', 'grp'), split_axis=0, concat_axis=0, til...]
    ppermute x5, waiting for transfers between devices: 0.1 us -> 16 us  [shifted(): return lax.ppermute(x, axis, pairs)]
    all_to_all x1 -> x0, starting transfers between devices: 12 us -> none  [local(): lax.all_to_all(outgoing, ('bin', 'grp'), split_axis=0, concat_axis=0, til...]
    ppermute x0 -> x5, starting transfers between devices: none -> 6.32 us  [arrange_tracks_by_axis(): d_next = lax.ppermute(mixed_arr, 'grp', line_up)]
    add x0 -> x4, other arithmetic: none -> 5.86 us  [arrange_tracks_by_axis(): mixed_arr = mixed_arr + d_next]
  transfers between devices with their start and end apart: 8 -> 11, of which waited for: 2 -> 4; matrix products, arithmetic and copies ran while one was open for 47% -> 50% of each run, Pallas kernels for 0% -> 0%
where the time goes in v1:
time: 480 us; the launch traced here: 471 us
  matrix products  174 us (36%)
  other arithmetic  82 us (17%)
  local copies, waits for them, and re-layouts  76.4 us (16%)
  waiting for transfers between devices  66.8 us (14%)
  blocking collectives  41.5 us (9%)
  starting transfers between devices  27.9 us (6%)
    conv_general_dilated x5, matrix products, filter_level(): lax.conv_general_dilated(joined[:, :, None], tap_rows[::-1][:, None, :],...  166 us
    ppermute x5, waiting for transfers between devices, arrange_tracks_by_axis(): d_next = lax.ppermute(mixed_arr, 'grp', line_up)  50.8 us
    all_to_all x1, blocking collectives, local(): lax.all_to_all(outgoing, ('bin', 'grp'), split_axis=0, concat_axis=0, til...  41.5 us
    another operation x6, other arithmetic, basis_from(): lower_factor = jnp.linalg.cholesky(inner_gram)  34.4 us
    another operation x3, other arithmetic, basis_from(): jax.scipy.linalg.solve_triangular(lower_factor, product.T, lower=True)  19.7 us
    ppermute x5, waiting for transfers between devices, shifted(): return lax.ppermute(x, axis, pairs)  16 us
    convert_element_type x6, local copies, waits for them, and re-layouts, local(): filtered.append(result_level.astype(jnp.bfloat16)[None])  15.2 us
    broadcast_in_dim x5, local copies, waits for them, and re-layouts, local(): filtered.append(result_level.astype(jnp.bfloat16)[None])  15.2 us
  transfers between devices with their start and end apart: 11, of which 4 were waited for; matrix products, arithmetic and copies ran while one was open for 50% of the time, Pallas kernels for 0%

profile of v1, /device:TPU:1, one launch (start us, length us, event | category | flops | bytes accessed | tf_op | source)
XLA Modules:
  0.0 471.4 jit_solution(12604310133420333948)
XLA Ops:
  2.4 6.9 %scatter_custom_fusion = bf16[2048,512]{1,0:T(8,128)(2,1)S(1)} fusion(s32[1024]{0:T(1024)S(1)} %bitcast.144, bf16[1024,512]{1,0:T(8,128)(2,1)} %param.6, f32[512]{0:T(512)S(1)} %bitcast.150, f32[512]{0:T(512)S(1)} %bitcast.151, f32[512]{0:T(512)S(1)} %bitcast.148, f32[512]{0:T(512)S(1)} %bitcast.149, f32[]{:T(128)} %constant.105.clone.1, ...), kind=kCustom, calls=%fused_computation.25 | custom fusion | flops 6291456 | bytes 3161094 | tf_op jit(solution)/shard_map/scatter | solution.py:87
  9.3 41.5 %all_to_all.24 = bf16[128,16,512]{2,1,0:T(8,128)(2,1)S(1)} all-to-all(bf16[128,16,512]{2,1,0:T(8,128)(2,1)S(1)} %bitcast.131), channel_id=1, replica_groups=mesh['bin'=4,'grp'=32] {'bin','grp'}, dimensions={0} | all-to-all | bytes 4194304 | tf_op jit(solution)/shard_map/all_to_all | solution.py:88
  55.5 6.4 %reshape.114 = f32[2,4096,2]{2,1,0:T(8,128)} reshape(f32[2,8192]{1,0:T(2,128)S(1)} %copy-done.8) | data formatting | bytes 131072 | tf_op jit(solution)/shard_map/reshape | solution.py:44
  61.9 5.9 %convert_reduce_fusion = bf16[2,4096]{1,0:T(2,128)(2,1)S(1)} fusion(f32[2,4096,2]{2,1,0:T(8,128)} %reshape.114), kind=kLoop, calls=%fused_computation.17 | loop fusion | flops 24576 | bytes 81920 | tf_op jit(solution)/shard_map/convert_element_type | solution.py:46
  77.2 3.7 collective-permute-start.7
  86.8 9.6 %collective-permute-done.1 = f32[512,512]{1,0:T(8,128)} collective-permute-done((f32[512,512]{1,0:T(8,128)}, f32[512,512]{1,0:T(8,128)}, u32[]{:S(2)}, u32[]{:S(2)}) %collective-permute-start.1) | collective-permute-done | bytes 1048608 | tf_op jit(solution)/shard_map/ppermute | solution.py:18
  107.1 16.0 %collective-permute-done.8 = bf16[2,64]{1,0:T(2,128)(2,1)S(1)} collective-permute-done((bf16[2,64]{1,0:T(2,128)(2,1)S(1)}, bf16[2,64]{1,0:T(2,128)(2,1)S(1)}, u32[]{:S(2)}, u32[]{:S(2)}) %collective-permute-start.8) | collective-permute-done | bytes 288 | tf_op jit(solution)/shard_map/ppermute | solution.py:27
  128.6 21.0 %collective-permute-done.3 = f32[512,512]{1,0:T(8,128)} collective-permute-done((f32[512,512]{1,0:T(8,128)S(1)}, f32[512,512]{1,0:T(8,128)}, u32[]{:S(2)}, u32[]{:S(2)}) %collective-permute-start.3) | collective-permute-done | bytes 1048608 | tf_op jit(solution)/shard_map/ppermute | solution.py:18
  155.2 20.2 %collective-permute-done.4 = f32[512,512]{1,0:T(8,128)} collective-permute-done((f32[512,512]{1,0:T(8,128)S(1)}, f32[512,512]{1,0:T(8,128)}, u32[]{:S(2)}, u32[]{:S(2)}) %collective-permute-start.4) | collective-permute-done | bytes 1048608 | tf_op jit(solution)/shard_map/ppermute | solution.py:18
  178.9 11.7 %cholesky.50 = f32[128,128]{1,0:T(8,128)S(1)} custom-call(f32[128,128]{1,0:T(8,128)S(1)} %cholesky.118), custom_call_target="Cholesky" | custom-call | tf_op jit(solution)/shard_map/jit(cholesky)/cholesky | solution.py:65
  190.7 9.8 %custom-call.15 = f32[1,128,128]{1,2,0:T(8,128)S(1)} custom-call(f32[1,128,128]{2,1,0:T(8,128)S(1)} %get-tuple-element.30), custom_call_target="InvertDiagBlocksLowerTriangular" | custom-call | tf_op jit(solution)/shard_map/jit(cholesky)/cholesky | solution.py:65
  201.0 12.2 %cholesky.105 = f32[128,128]{1,0:T(8,128)S(1)} custom-call(f32[128,128]{1,0:T(8,128)S(1)} %convolution_subtract_fusion), custom_call_target="Cholesky" | custom-call | tf_op jit(solution)/shard_map/jit(cholesky)/cholesky | solution.py:65
  215.2 4.0 while.1
  219.2 19.7 %custom-call.16 = f32[2,128,128]{1,2,0:T(8,128)S(1)} custom-call(f32[2,128,128]{2,1,0:T(8,128)S(1)} %get-tuple-element.14), custom_call_target="InvertDiagBlocksLowerTriangular" | custom-call | tf_op jit(solution)/shard_map/jit(_solve_triangular)/triangular_solve | solution.py:66
  241.3 6.6 %slice.147 = bf16[256,256]{0,1:T(8,128)(2,1)} slice(bf16[512,256]{0,1:T(8,128)(2,1)S(1)} %fusion.33), slice={[0:512:2], [0:256:1]} | slice | bytes 262144 | tf_op jit(solution)/shard_map/slice | solution.py:51
  255.8 8.2 %all-to-all-start.1 = ((bf16[128,16,256]{2,1,0:T(8,128)(2,1)}), bf16[128,16,256]{2,1,0:T(8,128)(2,1)}, u32[]{:S(2)}, u32[]{:S(2)}) async-start(bf16[128,16,256]{2,1,0:T(8,128)(2,1)} %bitcast.137), calls=%async_computation.1 | async-start | bytes 2097152 | tf_op jit(solution)/shard_map/all_to_all | solution.py:96
  267.3 123.0 %select_convert_fusion = bf16[16,1088,256]{2,0,1:T(8,128)(2,1)} fusion(pred[16,1088]{0,1:T(8,128)(4,1)S(1)} %bitcast.153, bf16[16,1599,1]{0,2,1:T(2,128)(2,1)S(1)} %copy-done.5, bf16[512,1,256]{2,1,0:T(2,128)(2,1)S(1)} %copy.51), kind=kOutput, calls=%fused_computation.5 | convolution fusion | flops 4572315648 | bytes 9243616 | tf_op jit(solution)/shard_map/conv_general_dilated | solution.py:53
  390.3 10.2 %copy.52 = bf16[16,1088,256]{2,1,0:T(8,128)(2,1)} copy(bf16[16,1088,256]{2,0,1:T(8,128)(2,1)} %select_convert_fusion) | data formatting | bytes 17825792 | tf_op jit(solution)/shard_map/convert_element_type | solution.py:109
  400.5 7.4 %slice_bitcast_fusion = bf16[1,2,8192,256]{3,2,1,0:T(8,128)(2,1)} fusion(bf16[2,8704,256]{2,1,0:T(8,128)(2,1)} %bitcast.127), kind=kLoop, calls=%fused_computation.7 | loop fusion | bytes 16777216 | tf_op jit(solution)/shard_map/broadcast_in_dim | solution.py:109
  408.5 31.3 %select_convert_fusion.1 = bf16[16,544,256]{2,0,1:T(8,128)(2,1)S(1)} fusion(pred[16,544]{0,1:T(8,128)(4,1)S(1)} %bitcast.154, bf16[16,799,1]{0,2,1:T(2,128)(2,1)S(1)} %copy-done.7, bf16[256,1,256]{2,1,0:T(2,128)(2,1)S(1)} %copy.54), kind=kOutput, calls=%fused_computation.6 | convolution fusion | flops 1145307136 | bytes 4621792 | tf_op jit(solution)/shard_map/conv_general_dilated | solution.py:53
  439.8 3.6 copy.55
  443.8 8.4 %select_convert_fusion.2 = bf16[16,272,256]{2,0,1:T(8,128)(2,1)S(1)} fusion(pred[16,272]{0,1:T(8,128)(4,1)S(1)} %copy-done.21, bf16[16,399,1]{0,2,1:T(2,128)(2,1)S(1)} %copy-done.12, bf16[128,1,256]{2,1,0:T(2,128)(2,1)S(1)} %copy.57), kind=kOutput, calls=%fused_computation.8 | convolution fusion | flops 287440896 | bytes 2310880 | tf_op jit(solution)/shard_map/conv_general_dilated | solution.py:53
  460.7 4.5 slice_bitcast_fusion.1
  465.2 6.0 %gather_fusion = bf16[1024,256]{1,0:T(8,128)(2,1)} fusion(bf16[2048,256]{1,0:T(8,128)(2,1)} %bitcast.22, s32[1024]{0:T(1024)S(1)} %copy-done.16), kind=kCustom, calls=%fused_computation | custom fusion | bytes 1052672 | tf_op jit(solution)/shard_map/gather | solution.py:97
  (183 shorter events, 74.9 us)
Async XLA Ops:
  0.6 174.7 %copy-start = (f32[512,256]{1,0:T(8,128)S(1)}, f32[512,256]{1,0:T(8,128)}, u32[]{:S(2)}) copy-start(f32[512,256]{1,0:T(8,128)} %param.10) | copy-start | bytes 1572868
  52.2 17.9 %collective-permute-start = (f32[512,512]{1,0:T(8,128)S(1)}, f32[512,512]{1,0:T(8,128)S(1)}, u32[]{:S(2)}, u32[]{:S(2)}) collective-permute-start(f32[512,512]{1,0:T(8,128)S(1)} %convolution_bitcast_fusion), channel_id=1, source_target_pairs={{0,1},{1,0},{2,3},{3,2},{4,5},{5,4},{6,7},{7,6},{8,9},{9,8},{10,11... | collective-permute-start | bytes 3145736 | tf_op jit(solution)/shard_map/ppermute | solution.py:18
  53.6 74.9 %collective-permute-start.5 = (bf16[2,512]{1,0:T(2,128)(2,1)S(1)}, bf16[2,512]{1,0:T(2,128)(2,1)S(1)}, u32[]{:S(2)}, u32[]{:S(2)}) collective-permute-start(bf16[2,512]{1,0:T(2,128)(2,1)S(1)} %slice.190), channel_id=1, source_target_pairs={{0,1},{1,2},{2,3},{3,4},{4,5},{5,6},{6,7},{7,8},{8,9},{9,10},{10,1... | collective-permute-start | bytes 6152 | tf_op jit(solution)/shard_map/ppermute | solution.py:27
  61.9 9.5 %copy-start.2 = (f32[2,4096,2]{2,1,0:T(8,128)S(1)}, f32[2,4096,2]{2,1,0:T(8,128)}, u32[]{:S(2)}) copy-start(f32[2,4096,2]{2,1,0:T(8,128)} %reshape.114) | copy-start | bytes 196612
  67.8 59.2 %collective-permute-start.6 = (bf16[2,256]{1,0:T(2,128)(2,1)S(1)}, bf16[2,256]{1,0:T(2,128)(2,1)S(1)}, u32[]{:S(2)}, u32[]{:S(2)}) collective-permute-start(bf16[2,256]{1,0:T(2,128)(2,1)S(1)} %slice.196), channel_id=1, source_target_pairs={{0,1},{1,2},{2,3},{3,4},{4,5},{5,6},{6,7},{7,8},{8,9},{9,10},{10,1... | collective-permute-start | bytes 3080 | tf_op jit(solution)/shard_map/ppermute | solution.py:27
  71.3 25.1 %collective-permute-start.1 = (f32[512,512]{1,0:T(8,128)}, f32[512,512]{1,0:T(8,128)}, u32[]{:S(2)}, u32[]{:S(2)}) collective-permute-start(f32[512,512]{1,0:T(8,128)} %add.100), channel_id=1, source_target_pairs={{0,2},{1,3},{2,0},{3,1},{4,6},{5,7},{6,4},{7,5},{8,10},{9,11},{10,... | collective-permute-start | bytes 3145736 | tf_op jit(solution)/shard_map/ppermute | solution.py:18
  77.2 47.0 %collective-permute-start.7 = (bf16[2,128]{1,0:T(2,128)(2,1)S(1)}, bf16[2,128]{1,0:T(2,128)(2,1)S(1)}, u32[]{:S(2)}, u32[]{:S(2)}) collective-permute-start(bf16[2,128]{1,0:T(2,128)(2,1)S(1)} %slice.202), channel_id=1, source_target_pairs={{0,1},{1,2},{2,3},{3,4},{4,5},{5,6},{6,7},{7,8},{8,9},{9,10},{10,1... | collective-permute-start | bytes 1544 | tf_op jit(solution)/shard_map/ppermute | solution.py:27
  84.8 17.7 %collective-permute-start.9 = (bf16[2,32]{1,0:T(2,128)(2,1)S(1)}, bf16[2,32]{1,0:T(2,128)(2,1)S(1)}, u32[]{:S(2)}, u32[]{:S(2)}) collective-permute-start(bf16[2,32]{1,0:T(2,128)(2,1)S(1)} %slice.212), channel_id=1, source_target_pairs={{0,1},{1,2},{2,3},{3,4},{4,5},{5,6},{6,7},{7,8},{8,9},{9,10},{10,1... | collective-permute-start | bytes 392 | tf_op jit(solution)/shard_map/ppermute | solution.py:27
  98.1 26.2 %collective-permute-start.2 = (f32[512,512]{1,0:T(8,128)S(1)}, f32[512,512]{1,0:T(8,128)}, u32[]{:S(2)}, u32[]{:S(2)}) collective-permute-start(f32[512,512]{1,0:T(8,128)S(1)} %add.101), channel_id=1, source_target_pairs={{0,4},{1,5},{2,6},{3,7},{4,0},{5,1},{6,2},{7,3},{8,12},{9,13},{10,... | collective-permute-start | bytes 3145736 | tf_op jit(solution)/shard_map/ppermute | solution.py:18
  102.5 20.6 %collective-permute-start.8 = (bf16[2,64]{1,0:T(2,128)(2,1)S(1)}, bf16[2,64]{1,0:T(2,128)(2,1)S(1)}, u32[]{:S(2)}, u32[]{:S(2)}) collective-permute-start(bf16[2,64]{1,0:T(2,128)(2,1)S(1)} %slice.207), channel_id=1, source_target_pairs={{0,1},{1,2},{2,3},{3,4},{4,5},{5,6},{6,7},{7,8},{8,9},{9,10},{10,1... | collective-permute-start | bytes 776 | tf_op jit(solution)/shard_map/ppermute | solution.py:27
  125.8 23.8 %collective-permute-start.3 = (f32[512,512]{1,0:T(8,128)S(1)}, f32[512,512]{1,0:T(8,128)}, u32[]{:S(2)}, u32[]{:S(2)}) collective-permute-start(f32[512,512]{1,0:T(8,128)S(1)} %add.102), channel_id=1, source_target_pairs={{0,8},{1,9},{2,10},{3,11},{4,12},{5,13},{6,14},{7,15},{8,0},{9,1},... | collective-permute-start | bytes 3145736 | tf_op jit(solution)/shard_map/ppermute | solution.py:18
  151.0 24.3 %collective-permute-start.4 = (f32[512,512]{1,0:T(8,128)S(1)}, f32[512,512]{1,0:T(8,128)}, u32[]{:S(2)}, u32[]{:S(2)}) collective-permute-start(f32[512,512]{1,0:T(8,128)S(1)} %add.103), channel_id=1, source_target_pairs={{0,16},{1,17},{2,18},{3,19},{4,20},{5,21},{6,22},{7,23},{8,24},{9,... | collective-permute-start | bytes 3145736 | tf_op jit(solution)/shard_map/ppermute | solution.py:18
  215.2 38.8 %copy-start.4 = (bf16[128,16,512]{2,1,0:T(8,128)(2,1)S(1)}, bf16[128,16,512]{2,1,0:T(8,128)(2,1)}, u32[]{:S(2)}) copy-start(bf16[128,16,512]{2,1,0:T(8,128)(2,1)} %copy-done.3) | copy-start | bytes 6291460
  255.8 11.5 %copy-start.5 = (bf16[16,1599,1]{0,2,1:T(2,128)(2,1)S(1)}, bf16[16,1599,1]{0,2,1:T(2,128)(2,1)}, u32[]{:S(2)}) copy-start(bf16[16,1599,1]{0,2,1:T(2,128)(2,1)} %copy.50) | copy-start | bytes 153508
  255.8 11.5 %copy-start.19 = (pred[16,1088]{0,1:T(32,128)(4,1)S(1)}, pred[16,1088]{0,1:T(32,128)(4,1)}, u32[]{:S(2)}) copy-start(pred[16,1088]{0,1:T(32,128)(4,1)} %constant.152) | copy-start | bytes 52228
  255.8 209.4 %all-to-all-start.1 = ((bf16[128,16,256]{2,1,0:T(8,128)(2,1)}), bf16[128,16,256]{2,1,0:T(8,128)(2,1)}, u32[]{:S(2)}, u32[]{:S(2)}) async-start(bf16[128,16,256]{2,1,0:T(8,128)(2,1)} %bitcast.137), calls=%async_computation.1 | async-start | bytes 2097152 | tf_op jit(solution)/shard_map/all_to_all | solution.py:96
  400.5 7.4 %copy-start.6 = (bf16[256,256]{0,1:T(8,128)(2,1)S(1)}, bf16[256,256]{0,1:T(8,128)(2,1)}, u32[]{:S(2)}) copy-start(bf16[256,256]{0,1:T(8,128)(2,1)} %slice.147) | copy-start | bytes 393220
  400.5 8.0 %copy-start.7 = (bf16[16,799,1]{0,2,1:T(2,128)(2,1)S(1)}, bf16[16,799,1]{0,2,1:T(2,128)(2,1)}, u32[]{:S(2)}) copy-start(bf16[16,799,1]{0,2,1:T(2,128)(2,1)} %copy.53) | copy-start | bytes 76708
  400.5 8.0 %copy-start.20 = (pred[16,544]{0,1:T(32,128)(4,1)S(1)}, pred[16,544]{0,1:T(32,128)(4,1)}, u32[]{:S(2)}) copy-start(pred[16,544]{0,1:T(32,128)(4,1)} %constant.153) | copy-start | bytes 26116
  439.8 3.7 copy-start.11
  439.8 4.0 copy-start.12
  439.8 4.0 copy-start.21
  460.7 4.5 copy-start.16
  465.2 6.0 %copy-start.1 = (f32[512,256]{1,0:T(8,128)S(1)}, f32[512,256]{1,0:T(8,128)}, u32[]{:S(2)}) copy-start(f32[512,256]{1,0:T(8,128)} %param.10) | copy-start | bytes 1572868
  (11 other events, 18.6 us)
